TPU v7x, 256 devices: a whole 4x4x8 slice. The times are simulated.
256 devices in a mesh: row: 8 (over y_lo, x), col: 16 (over z, core), layer: 2 (over y_hi).
Axes of the slice: x: 4, y: 4 (y_hi: 2, y_lo: 2; y = y_hi * 2 + y_lo), z: 8, core: 2. Of those that a mesh axis runs over, the one named last changes fastest.
Arguments:
- basis_left: bfloat16 [32768, 32, 128], P(('row', 'col', 'layer')), may hold values from -6 to 6
- basis_right: bfloat16 [32768, 32, 128], P(('row', 'col', 'layer')), may hold values from -6 to 6
- grid_weight: float32 [32768, 128], P(('row', 'col', 'layer')), may hold values from -0.3 to 0.3
- task_owner: int32 [32768, 1], P(('row', 'col', 'layer')), may hold values from 0 to 127; in each aligned block of 128 rows (0 to 127, 128 to 255, ...) at most 2 rows name the same one
- task_block: int32 [32768], P(('row', 'col', 'layer')), may hold values from 0 to 511
- core_matrix: float32 [8192, 8192], P('row', 'col'), may hold values from -6 to 6
- block_mask: int32 [256, 256], P('row', 'col'), may hold values 0 or 1
Outputs:
- ks_matrix: float32 [8192, 8192], P('row', ('col', 'layer'))
- density: float32 [8192, 8192], P('row', ('col', 'layer'))
Inputs may be any that keep to these rules, and one draw needn't show every extreme that they name: `task_owner`: in the tasks of one device no owner is named more than 2 times, a bound that some block reaches.
All inputs are finite; a program needn't handle non-finite values. No bound on the sum of `block_mask` on one device may be relied on, other than what follows from the above.
Results may differ from a plain program's by a relative error of at most 0.0053.
Values may be sent and summed in bfloat16 or wider, within the bound.
No kernel may reach another device: no remote copies, remote signals or barrier semaphores. Data moves between devices by JAX's collectives and lax.ppermute only.
A program may use at most 128 MiB of HBM per device.

v0:
```python
import math
import jax
import jax.numpy as jnp
from jax import lax
from jax.sharding import PartitionSpec as P

BS = 32
NBLK = 256
COUPLING = 2.5


def local(basis_left, basis_right, grid_weight, task_owner, task_block, core_matrix, block_mask):
    rows_local, panel_width = core_matrix.shape
    layers = lax.axis_size("layer")
    row_count = lax.axis_size("row")
    col_count = lax.axis_size("col")
    owners = row_count * col_count
    subwidth = panel_width // layers
    matrix_order = NBLK * BS
    block_rows = NBLK // row_count
    block_cols = NBLK // col_count
    owned_blocks = block_rows * block_cols
    task_count = basis_left.shape[0]
    capacity = max(2, 2 * task_count // owners)
    row_index = lax.axis_index("row")
    col_index = lax.axis_index("col")
    layer_index = lax.axis_index("layer")
    weighted = (basis_left * grid_weight[:, None, :]).astype(jnp.bfloat16)
    blocks = jnp.einsum("tag,tbg->tab", weighted, basis_right, preferred_element_type=jnp.float32)
    blocks = blocks.reshape(task_count, BS * BS)
    target = task_owner[:, 0]
    onehot = (target[:, None] == jnp.arange(owners, dtype=jnp.int32)[None, :]).astype(jnp.int32)
    before = jnp.cumsum(onehot, axis=0) - onehot
    slot_index = jnp.sum(before * onehot, axis=1)
    position = target * capacity + slot_index
    outgoing = jnp.zeros((owners * capacity, BS * BS), jnp.float32).at[position].set(blocks)
    labels = (
        jnp.full((owners * capacity,), float(owned_blocks), jnp.float32)
        .at[position]
        .set(task_block.astype(jnp.float32))
    )
    arrived, arrived_ids = (
        lax.all_to_all(
            outgoing.reshape(owners, capacity, BS * BS),
            ("row", "col"),
            split_axis=0,
            concat_axis=0,
            tiled=True,
        ),
        lax.all_to_all(
            labels.reshape(owners, capacity),
            ("row", "col"),
            split_axis=0,
            concat_axis=0,
            tiled=True,
        ),
    )
    collected = (
        jnp.zeros((owned_blocks, BS * BS), jnp.float32)
        .at[arrived_ids.reshape(-1).astype(jnp.int32)]
        .add(arrived.reshape(-1, BS * BS), mode="drop")
    )
    local_panel = (
        collected.reshape(block_rows, block_cols, BS, BS)
        .transpose(0, 2, 1, 3)
        .reshape(rows_local, panel_width)
    )
    block_row_ids = row_index * block_rows + jnp.arange(block_rows, dtype=jnp.int32)
    block_col_ids = col_index * block_cols + jnp.arange(block_cols, dtype=jnp.int32)
    pattern_blocks = (block_mask != 0) | (block_row_ids[:, None] == block_col_ids[None, :])
    pattern = jnp.repeat(jnp.repeat(pattern_blocks.astype(jnp.float32), BS, 0), BS, 1)
    global_row = row_index * rows_local + jnp.arange(rows_local, dtype=jnp.int32)
    global_col = col_index * panel_width + jnp.arange(panel_width, dtype=jnp.int32)
    identity = (global_row[:, None] == global_col[None, :]).astype(jnp.float32)
    coupling_scale = COUPLING / math.sqrt(matrix_order)

    def own_columns(panel):
        return lax.dynamic_index_in_dim(
            panel.reshape(rows_local, layers, subwidth), layer_index, axis=1, keepdims=False
        )

    grid_terms = lax.psum_scatter(local_panel, "layer", scatter_dimension=1, tiled=True)
    ks_out = own_columns(core_matrix) + grid_terms
    pattern_own = own_columns(pattern)
    identity_own = own_columns(identity)
    initial = (pattern_own * (0.5 * identity_own - coupling_scale * ks_out)).astype(jnp.bfloat16)
    column_panel = lax.all_gather(initial, "row", axis=0, tiled=True)

    def accumulate(incoming):
        return jnp.dot(incoming, column_panel, preferred_element_type=jnp.float32)

    square = pattern_own * accumulate(lax.all_gather(initial, ("col", "layer"), axis=1, tiled=True))
    cube_term = pattern_own * accumulate(
        lax.all_gather(square.astype(jnp.bfloat16), ("col", "layer"), axis=1, tiled=True)
    )
    density = 3.0 * square - 2.0 * cube_term
    return (ks_out, density)


def solution(mesh):
    placed = (
        P(("row", "col", "layer"), None, None),
        P(("row", "col", "layer"), None, None),
        P(("row", "col", "layer"), None),
        P(("row", "col", "layer"), None),
        P(("row", "col", "layer")),
        P("row", "col"),
        P("row", "col"),
    )
    return jax.shard_map(
        local,
        mesh=mesh,
        in_specs=placed,
        out_specs=(P("row", ("col", "layer")), P("row", ("col", "layer"))),
        check_vma=False,
    )
```

profile of v0, /device:TPU:1, one launch (start us, length us, event | category | flops | bytes accessed | tf_op | source)
XLA Modules:
  0.0 535.9 jit_solution(16276669535692589134)
XLA Ops:
  10.3 1.0 scatter_custom_fusion
  12.1 14.8 %all-to-all-start = ((f32[128,1,2]{2,1,0:T(1,128)}), f32[128,1,2]{2,1,0:T(1,128)S(1)}, u32[]{:S(2)}, u32[]{:S(2)}) async-start(f32[128,1,2]{2,1,0:T(1,128)} %bitcast.4), calls=%async_computation | async-start | bytes 131072 | tf_op jit(solution)/shard_map/all_to_all | solution.py:50
  26.9 1.9 fusion.2
  28.8 1.3 copy.22
  30.3 1.3 scatter_custom_fusion.1
  31.5 1.6 reshape.84
  33.1 4.3 all-to-all-done
  37.4 8.1 %all-to-all-start.1 = ((f32[128,2,1024]{2,1,0:T(2,128)}), f32[128,2,1024]{2,1,0:T(2,128)S(1)}, u32[]{:S(2)}, u32[]{:S(2)}) async-start(f32[128,2,1024]{2,1,0:T(2,128)} %reshape.84), calls=%async_computation.1 | async-start | bytes 2097152 | tf_op jit(solution)/shard_map/all_to_all | solution.py:43
  46.0 28.4 %all-to-all-done.1 = f32[128,2,1024]{2,1,0:T(2,128)S(1)} async-done(((f32[128,2,1024]{2,1,0:T(2,128)}), f32[128,2,1024]{2,1,0:T(2,128)S(1)}, u32[]{:S(2)}, u32[]{:S(2)}) %all-to-all-start.1) | async-done | bytes 1048608 | tf_op jit(solution)/shard_map/all_to_all | solution.py:43
  74.4 1.7 reshape.109
  76.1 4.0 scatter_custom_fusion.2
  80.1 4.8 reshape.86
  84.8 14.2 %copy.24 = f32[32,32,16,32]{3,2,1,0:T(8,128)} copy(f32[32,32,16,32]{3,1,2,0:T(8,128)} %bitcast.38) | data formatting | bytes 4194304 | tf_op jit(solution)/shard_map/transpose | solution.py:65
  99.0 7.3 %reshape.87 = f32[1024,512]{1,0:T(8,128)} reshape(f32[32,32,16,32]{3,2,1,0:T(8,128)} %copy.24) | data formatting | bytes 4194304 | tf_op jit(solution)/shard_map/reshape | solution.py:66
  107.4 1.3 copy.25
  108.7 2.6 reshape.82
  111.3 0.9 constant_dynamic-slice_fusion.2
  112.2 30.3 %reduce-scatter.2.cloned.1.call-done = f32[1024,256]{1,0:T(8,128)} async-done(((f32[1024,512]{1,0:T(8,128)}), f32[1024,256]{1,0:T(8,128)}) %reduce-scatter.2.cloned.1.call-update) | async-done | bytes 1048592 | tf_op jit(solution)/shard_map/reduce_scatter | solution.py:82
  142.4 3.0 fusion.5
  146.2 53.9 %all-gather.6.cloned.1.call-done = bf16[8192,256]{1,0:T(8,128)(2,1)} async-done(((bf16[1024,256]{1,0:T(8,128)(2,1)}), bf16[8192,256]{1,0:T(8,128)(2,1)}) %all-gather.6.cloned.1.call-update) | async-done | bytes 4194320 | tf_op jit(solution)/shard_map/all_gather | solution.py:87
  200.1 154.9 %all-gather.4.cloned.1.call-done = bf16[1024,8192]{1,0:T(8,128)(2,1)} async-done(((bf16[1024,256]{1,0:T(8,128)(2,1)}), bf16[1024,8192]{1,0:T(8,128)(2,1)}) %all-gather.4.cloned.1.call-update) | async-done | bytes 16777232 | tf_op jit(solution)/shard_map/all_gather | solution.py:92
  355.0 12.5 %fusion.16 = (bf16[1024,256]{1,0:T(8,128)(2,1)}, f32[1024,256]{1,0:T(8,128)S(1)}) fusion(bf16[1024,8192]{1,0:T(8,128)(2,1)} %all-gather.4.cloned.1.call-done, bf16[8192,256]{1,0:T(8,128)(2,1)} %all-gather.6.cloned.1.call-done, f32[1024,1,256]{2,0,1:T(8,128)} %copy.25), kind=kOutput, calls=%fused_computation.37 | convolution fusion | flops 4295491584 | bytes 23592960 | tf_op jit(solution)/shard_map/dot_general | solution.py:90
  367.6 149.2 %all-gather.8.cloned.1.call-done = bf16[1024,8192]{1,0:T(8,128)(2,1)} async-done(((bf16[1024,256]{1,0:T(8,128)(2,1)}), bf16[1024,8192]{1,0:T(8,128)(2,1)}) %all-gather.8.cloned.1.call-update) | async-done | bytes 16777232 | tf_op jit(solution)/shard_map/all_gather | solution.py:94
  516.8 12.5 %fusion.1 = f32[1024,256]{1,0:T(8,128)} fusion(bf16[1024,8192]{1,0:T(8,128)(2,1)} %all-gather.8.cloned.1.call-done, bf16[8192,256]{1,0:T(8,128)(2,1)} %all-gather.6.cloned.1.call-done, f32[1024,1,256]{2,0,1:T(8,128)S(1)} %copy-done.2, f32[1024,256]{1,0:T(8,128)S(1)} %get-tuple-element.5), kind=kOutput, calls=%fused_computation.7 | convolution fusion | flops 4296015872 | bytes 24117248 | tf_op jit(solution)/shard_map/dot_general | solution.py:90
  (36 shorter events, 6.3 us)
Async XLA Ops:
  7.2 19.7 %copy-start = (bf16[128,32,128]{2,1,0:T(8,128)(2,1)S(1)}, bf16[128,32,128]{2,1,0:T(8,128)(2,1)}, u32[]{:S(2)}) copy-start(bf16[128,32,128]{2,1,0:T(8,128)(2,1)} %param.8) | copy-start | bytes 3145732
  12.1 25.4 %all-to-all-start = ((f32[128,1,2]{2,1,0:T(1,128)}), f32[128,1,2]{2,1,0:T(1,128)S(1)}, u32[]{:S(2)}, u32[]{:S(2)}) async-start(f32[128,1,2]{2,1,0:T(1,128)} %bitcast.4), calls=%async_computation | async-start | bytes 131072 | tf_op jit(solution)/shard_map/all_to_all | solution.py:50
  37.4 36.9 %all-to-all-start.1 = ((f32[128,2,1024]{2,1,0:T(2,128)}), f32[128,2,1024]{2,1,0:T(2,128)S(1)}, u32[]{:S(2)}, u32[]{:S(2)}) async-start(f32[128,2,1024]{2,1,0:T(2,128)} %reshape.84), calls=%async_computation.1 | async-start | bytes 2097152 | tf_op jit(solution)/shard_map/all_to_all | solution.py:43
  45.6 96.9 %reduce-scatter.2.cloned.1.call-start = ((), (), s32[]{:S(2)}) async-start(), calls=%async_computation.3 | async-start | bytes 3145728 | tf_op jit(solution)/shard_map/reduce_scatter | solution.py:82
  99.0 7.7 %copy-start.3 = (s32[32,16]{0,1:T(8,128)S(1)}, s32[32,16]{0,1:T(8,128)}, u32[]{:S(2)}) copy-start(s32[32,16]{0,1:T(8,128)} %param.13) | copy-start | bytes 6148
  106.3 93.8 %all-gather.6.cloned.1.call-start = ((), (), s32[]{:S(2)}) async-start(), calls=%async_computation.5 | async-start | bytes 4718592 | tf_op jit(solution)/shard_map/all_gather | solution.py:87
  145.4 209.6 %all-gather.4.cloned.1.call-start = ((), (), s32[]{:S(2)}) async-start(), calls=%async_computation.4 | async-start | bytes 17301504 | tf_op jit(solution)/shard_map/all_gather | solution.py:92
  146.2 370.6 %copy-start.2 = (f32[1024,1,256]{2,0,1:T(8,128)S(1)}, f32[1024,1,256]{2,0,1:T(8,128)}, u32[]{:S(2)}) copy-start(f32[1024,1,256]{2,0,1:T(8,128)} %copy.25) | copy-start | bytes 3145732
  146.2 370.6 %all-gather.8.cloned.1.call-start = ((), (), s32[]{:S(2)}) async-start(), calls=%async_computation.6 | async-start | bytes 17301504 | tf_op jit(solution)/shard_map/all_gather | solution.py:94
  516.8 12.5 %copy-start.1 = (bf16[128,32,128]{2,1,0:T(8,128)(2,1)S(1)}, bf16[128,32,128]{2,1,0:T(8,128)(2,1)}, u32[]{:S(2)}) copy-start(bf16[128,32,128]{2,1,0:T(8,128)(2,1)} %param.8) | copy-start | bytes 3145732
Sparse Core Ops, SparseCore 0:
  106.5 35.9 reduce-scatter.1
  145.6 54.5 all-gather.5
  203.0 151.9 all-gather.3
  367.7 149.0 all-gather.7
where the time goes:
time: 536 us
  waiting for transfers between devices  422 us (79%)
  local copies, waits for them, and re-layouts  39.6 us (7%)
  matrix products  26.9 us (5%)
  starting transfers between devices  23.3 us (4%)
  between operations  14 us (3%)
  other arithmetic  10.4 us (2%)
    all_gather x1, waiting for transfers between devices, local(): lax.all_gather(initial, ('col', 'layer'), axis=1, tiled=True)  155 us
    all_gather x1, waiting for transfers between devices, local(): lax.all_gather(square.astype(jnp.bfloat16), ('col', 'layer'), axis=1, til...  149 us
    all_gather x1, waiting for transfers between devices, local(): column_panel = lax.all_gather(initial, 'row', axis=0, tiled=True)  53.9 us
    reduce_scatter x1, waiting for transfers between devices, local(): lax.psum_scatter(local_panel, 'layer', scatter_dimension=1, tiled=True)  30.3 us
    all_to_all x1, waiting for transfers between devices, local(): lax.all_to_all(outgoing.reshape(owners, capacity, BS * BS), ('row', 'col'...  28.4 us
    dot_general x2, matrix products, accumulate(): return jnp.dot(incoming, column_panel, preferred_element_type=jnp.float32)  25.1 us
    all_to_all x1, starting transfers between devices, local(): lax.all_to_all(labels.reshape(owners, capacity), ('row', 'col'), split_ax...  14.8 us
    transpose x1, local copies, waits for them, and re-layouts, local(): local_panel = collected.reshape(block_rows, block_cols, BS, BS).transpose...  14.2 us
  transfers between devices with their start and end apart: 6, of which 6 were waited for; matrix products, arithmetic and copies ran while one was open for 2% of the time, Pallas kernels for 0%

commit v1 on v0

--- a/solution.py
+++ b/solution.py
@@ -84,7 +84,9 @@
     pattern_own = own_columns(pattern)
     identity_own = own_columns(identity)
     initial = (pattern_own * (0.5 * identity_own - coupling_scale * ks_out)).astype(jnp.bfloat16)
-    column_panel = lax.all_gather(initial, "row", axis=0, tiled=True)
+    column_panel = jnp.concatenate(
+        lax.all_to_all(jnp.stack([initial] * lax.axis_size("row")), "row", 0, 0), axis=0
+    )
 
     def accumulate(incoming):
         return jnp.dot(incoming, column_panel, preferred_element_type=jnp.float32)

time: 536 us -> 514 us (0.959)
  waiting for transfers between devices: 422 us -> 342 us
  blocking collectives: 0 us -> 56.1 us
    all_to_all x0 -> x1, blocking collectives: none -> 56.1 us  [local(): lax.all_to_all(jnp.stack([initial] * lax.axis_size('row')), 'row', 0, 0)]
    all_gather x1 -> x0, waiting for transfers between devices: 53.9 us -> none  [local(): column_panel = lax.all_gather(initial, 'row', axis=0, tiled=True)]
    all_gather x1, waiting for transfers between devices: 155 us -> 129 us  [local(): lax.all_gather(initial, ('col', 'layer'), axis=1, tiled=True)]
  transfers between devices with their start and end apart: 6 -> 5, of which waited for: 6 -> 5; matrix products, arithmetic and copies ran while one was open for 2% -> 3% of each run, Pallas kernels for 0% -> 0%
where the time goes in v1:
time: 514 us; the launch traced here: 513 us
  waiting for transfers between devices  342 us (67%)
  blocking collectives  56.1 us (11%)
  local copies, waits for them, and re-layouts  40.9 us (8%)
  matrix products  26.6 us (5%)
  starting transfers between devices  23.3 us (5%)
  between operations  14 us (3%)
  other arithmetic  10.4 us (2%)
    all_gather x1, waiting for transfers between devices, local(): lax.all_gather(square.astype(jnp.bfloat16), ('col', 'layer'), axis=1, til...  149 us
    all_gather x1, waiting for transfers between devices, local(): lax.all_gather(initial, ('col', 'layer'), axis=1, tiled=True)  129 us
    all_to_all x1, blocking collectives, local(): lax.all_to_all(jnp.stack([initial] * lax.axis_size('row')), 'row', 0, 0)  56.1 us
    reduce_scatter x1, waiting for transfers between devices, local(): lax.psum_scatter(local_panel, 'layer', scatter_dimension=1, tiled=True)  30.3 us
    all_to_all x1, waiting for transfers between devices, local(): lax.all_to_all(outgoing.reshape(owners, capacity, BS * BS), ('row', 'col'...  28.4 us
    dot_general x2, matrix products, accumulate(): return jnp.dot(incoming, column_panel, preferred_element_type=jnp.float32)  24.8 us
    all_to_all x1, starting transfers between devices, local(): lax.all_to_all(labels.reshape(owners, capacity), ('row', 'col'), split_ax...  14.8 us
    transpose x1, local copies, waits for them, and re-layouts, local(): local_panel = collected.reshape(block_rows, block_cols, BS, BS).transpose...  14.2 us
  transfers between devices with their start and end apart: 5, of which 5 were waited for; matrix products, arithmetic and copies ran while one was open for 3% of the time, Pallas kernels for 0%

profile of v1, /device:TPU:1, one launch (start us, length us, event | category | flops | bytes accessed | tf_op | source)
XLA Modules:
  0.0 512.9 jit_solution(7955135764376656257)
XLA Ops:
  10.3 1.0 scatter_custom_fusion
  12.1 14.8 %all-to-all-start = ((f32[128,1,2]{2,1,0:T(1,128)}), f32[128,1,2]{2,1,0:T(1,128)S(1)}, u32[]{:S(2)}, u32[]{:S(2)}) async-start(f32[128,1,2]{2,1,0:T(1,128)} %bitcast.4), calls=%async_computation | async-start | bytes 131072 | tf_op jit(solution)/shard_map/all_to_all | solution.py:50
  26.9 1.9 fusion.2
  28.8 1.3 copy.22
  30.3 1.3 scatter_custom_fusion.1
  31.5 1.6 reshape.89
  33.1 4.3 all-to-all-done
  37.4 8.1 %all-to-all-start.1 = ((f32[128,2,1024]{2,1,0:T(2,128)}), f32[128,2,1024]{2,1,0:T(2,128)S(1)}, u32[]{:S(2)}, u32[]{:S(2)}) async-start(f32[128,2,1024]{2,1,0:T(2,128)} %reshape.89), calls=%async_computation.1 | async-start | bytes 2097152 | tf_op jit(solution)/shard_map/all_to_all | solution.py:43
  46.0 28.4 %all-to-all-done.1 = f32[128,2,1024]{2,1,0:T(2,128)S(1)} async-done(((f32[128,2,1024]{2,1,0:T(2,128)}), f32[128,2,1024]{2,1,0:T(2,128)S(1)}, u32[]{:S(2)}, u32[]{:S(2)}) %all-to-all-start.1) | async-done | bytes 1048608 | tf_op jit(solution)/shard_map/all_to_all | solution.py:43
  74.4 1.7 reshape.115
  76.1 4.0 scatter_custom_fusion.2
  80.1 4.8 reshape.91
  84.9 14.2 %copy.24 = f32[32,32,16,32]{3,2,1,0:T(8,128)} copy(f32[32,32,16,32]{3,1,2,0:T(8,128)} %bitcast.37) | data formatting | bytes 4194304 | tf_op jit(solution)/shard_map/transpose | solution.py:65
  99.0 7.3 %reshape.92 = f32[1024,512]{1,0:T(8,128)} reshape(f32[32,32,16,32]{3,2,1,0:T(8,128)} %copy.24) | data formatting | bytes 4194304 | tf_op jit(solution)/shard_map/reshape | solution.py:66
  107.4 1.3 copy.25
  108.7 2.6 reshape.87
  112.2 30.3 %reduce-scatter.2.cloned.1.call-done = f32[1024,256]{1,0:T(8,128)} async-done(((f32[1024,512]{1,0:T(8,128)}), f32[1024,256]{1,0:T(8,128)}) %reduce-scatter.2.cloned.1.call-update) | async-done | bytes 1048592 | tf_op jit(solution)/shard_map/reduce_scatter | solution.py:82
  142.5 3.0 fusion.5
  145.6 1.3 stack.2
  146.9 56.1 %all_to_all.19 = bf16[8,1024,256]{2,1,0:T(8,128)(2,1)} all-to-all(bf16[8,1024,256]{2,1,0:T(8,128)(2,1)S(1)} %stack.2), channel_id=1, replica_groups=mesh['row'=8,'col'=16,'layer'=2] {'row'}, dimensions={0} | all-to-all | bytes 8388608 | tf_op jit(solution)/shard_map/all_to_all | solution.py:88
  203.0 129.4 %all-gather.3.cloned.1.call-done = bf16[1024,8192]{1,0:T(8,128)(2,1)} async-done(((bf16[1024,256]{1,0:T(8,128)(2,1)}), bf16[1024,8192]{1,0:T(8,128)(2,1)}) %all-gather.3.cloned.1.call-update) | async-done | bytes 16777232 | tf_op jit(solution)/shard_map/all_gather | solution.py:94
  332.4 12.2 %fusion.16 = (bf16[1024,256]{1,0:T(8,128)(2,1)}, f32[1024,256]{1,0:T(8,128)S(1)}) fusion(bf16[1024,8192]{1,0:T(8,128)(2,1)} %all-gather.3.cloned.1.call-done, bf16[8192,256]{1,0:T(8,128)(2,1)} %bitcast.39, f32[1024,1,256]{2,0,1:T(8,128)S(1)} %copy-done.2), kind=kOutput, calls=%fused_computation.37 | convolution fusion | flops 4295491584 | bytes 23592960 | tf_op jit(solution)/shard_map/dot_general | solution.py:92
  344.7 149.2 %all-gather.5.cloned.1.call-done = bf16[1024,8192]{1,0:T(8,128)(2,1)} async-done(((bf16[1024,256]{1,0:T(8,128)(2,1)}), bf16[1024,8192]{1,0:T(8,128)(2,1)}) %all-gather.5.cloned.1.call-update) | async-done | bytes 16777232 | tf_op jit(solution)/shard_map/all_gather | solution.py:96
  493.9 12.5 %fusion.1 = f32[1024,256]{1,0:T(8,128)} fusion(bf16[1024,8192]{1,0:T(8,128)(2,1)} %all-gather.5.cloned.1.call-done, bf16[8192,256]{1,0:T(8,128)(2,1)} %bitcast.40, f32[1024,1,256]{2,0,1:T(8,128)S(1)} %copy-done.2, f32[1024,256]{1,0:T(8,128)S(1)} %get-tuple-element.5), kind=kOutput, calls=%fused_computation.7 | convolution fusion | flops 4296015872 | bytes 24117248 | tf_op jit(solution)/shard_map/dot_general | solution.py:92
  (35 shorter events, 6.5 us)
Async XLA Ops:
  7.2 19.7 %copy-start = (bf16[128,32,128]{2,1,0:T(8,128)(2,1)S(1)}, bf16[128,32,128]{2,1,0:T(8,128)(2,1)}, u32[]{:S(2)}) copy-start(bf16[128,32,128]{2,1,0:T(8,128)(2,1)} %param.8) | copy-start | bytes 3145732
  12.1 25.4 %all-to-all-start = ((f32[128,1,2]{2,1,0:T(1,128)}), f32[128,1,2]{2,1,0:T(1,128)S(1)}, u32[]{:S(2)}, u32[]{:S(2)}) async-start(f32[128,1,2]{2,1,0:T(1,128)} %bitcast.4), calls=%async_computation | async-start | bytes 131072 | tf_op jit(solution)/shard_map/all_to_all | solution.py:50
  37.4 36.9 %all-to-all-start.1 = ((f32[128,2,1024]{2,1,0:T(2,128)}), f32[128,2,1024]{2,1,0:T(2,128)S(1)}, u32[]{:S(2)}, u32[]{:S(2)}) async-start(f32[128,2,1024]{2,1,0:T(2,128)} %reshape.89), calls=%async_computation.1 | async-start | bytes 2097152 | tf_op jit(solution)/shard_map/all_to_all | solution.py:43
  45.6 96.9 %reduce-scatter.2.cloned.1.call-start = ((), (), s32[]{:S(2)}) async-start(), calls=%async_computation.4 | async-start | bytes 3145728 | tf_op jit(solution)/shard_map/reduce_scatter | solution.py:82
  99.0 7.7 %copy-start.3 = (s32[32,16]{0,1:T(8,128)S(1)}, s32[32,16]{0,1:T(8,128)}, u32[]{:S(2)}) copy-start(s32[32,16]{0,1:T(8,128)} %param.13) | copy-start | bytes 6148
  106.4 226.0 %all-gather.3.cloned.1.call-start = ((), (), s32[]{:S(2)}) async-start(), calls=%async_computation.5 | async-start | bytes 17301504 | tf_op jit(solution)/shard_map/all_gather | solution.py:94
  145.5 348.4 %all-gather.5.cloned.1.call-start = ((), (), s32[]{:S(2)}) async-start(), calls=%async_computation.6 | async-start | bytes 17301504 | tf_op jit(solution)/shard_map/all_gather | solution.py:96
  146.9 185.5 %copy-start.2 = (f32[1024,1,256]{2,0,1:T(8,128)S(1)}, f32[1024,1,256]{2,0,1:T(8,128)}, u32[]{:S(2)}) copy-start(f32[1024,1,256]{2,0,1:T(8,128)} %copy.25) | copy-start | bytes 3145732
  493.9 12.5 %copy-start.1 = (bf16[128,32,128]{2,1,0:T(8,128)(2,1)S(1)}, bf16[128,32,128]{2,1,0:T(8,128)(2,1)}, u32[]{:S(2)}) copy-start(bf16[128,32,128]{2,1,0:T(8,128)(2,1)} %param.8) | copy-start | bytes 3145732
Sparse Core Ops, SparseCore 0:
  106.5 35.9 reduce-scatter.1
  145.6 186.7 all-gather.2
  344.8 149.0 all-gather.4
